TPU v7x, 512 devices: a whole 4x8x8 slice. The times are simulated.
512 devices in a mesh: rows: 32 (over x, z), cols: 16 (over y, core).
Axes of the slice: x: 4, y: 8, z: 8, core: 2. Of those that a mesh axis runs over, the one named last changes fastest.
Arguments:
- points: float32 [3, 131072], P(None, 'rows'), as said below
- targets: float32 [16, 131072], P(None, 'rows'), may hold values from -6 to 6
- landmarks: int32 [256], replicated, may hold values from 0 to 131071
- neighbours: int32 [1024, 18], P('rows'), may hold values from 0 to 1023, as said below
- counts: int32 [1024], P('rows'), may hold values from 1 to 18
- core_inverse: float32 [256, 256], replicated, as said below
Outputs:
- solution: float32 [16, 131072], P(None, 'rows')
- residual: float32 [16, 131072], P(None, 'rows')
Inputs may be any that keep to these rules, and one draw needn't show every extreme that they name: `neighbours`: for block b the first counts[b] entries are distinct blocks in ascending order, b among them, each within 12 blocks of b; b lists c exactly when c lists b; the remaining slots hold b. `points`: points of blocks that do not list each other are farther apart than 1. `core_inverse`: Symmetric; each diagonal entry exceeds the sum of the magnitudes of the other entries of its row.
All inputs are finite; a program needn't handle non-finite values.
Results may differ from a plain program's by a relative error of at most 0.0003.
Values sent between devices are 32-bit elements; how exact they have to be, the bound alone decides.
A program may use at most 64 MiB of HBM per device.

v0:
```python
import jax
import jax.numpy as jnp
from jax import lax
from jax.sharding import PartitionSpec as P

MOST = 6
ITERS = 2
kernel_scale = 0.03125
ridge_shift = 1.0
tile_group = 32


def extended(cells, sides, width):
    for axis, dim in sides:
        count = lax.axis_size(axis)
        ends = count - 1
        head = lax.slice_in_dim(cells, 0, width, axis=dim)
        tail = lax.slice_in_dim(cells, cells.shape[dim] - width, cells.shape[dim], axis=dim)
        cells = jnp.concatenate(
            [
                lax.ppermute(tail, axis, [(i, (i + 1) % count) for i in range(ends)]),
                cells,
                lax.ppermute(head, axis, [((i + 1) % count, i) for i in range(ends)]),
            ],
            axis=dim,
        )
    return cells


def wendland(squared):
    distance = jnp.sqrt(squared)
    remain = jnp.maximum(1.0 - distance, 0.0)
    return remain * remain * remain * remain * (4.0 * distance + 1.0)


def squared_gap(first_pts, second_pts):
    offsets = first_pts[:, :, None] - second_pts[:, None, :]
    return jnp.sum(offsets * offsets, axis=0)


def tile_products(vector_halo, point_halo, row_points, nearby, amounts, last_tile):
    block_count = row_points.shape[1]
    block_width = row_points.shape[2]
    slot_count = nearby.shape[1]
    tile_ends = jnp.cumsum(amounts)
    tile_starts = tile_ends - amounts
    lane_ids = jnp.arange(tile_group, dtype=jnp.int32)
    block_ids = jnp.arange(block_count, dtype=jnp.int32)
    turn_count = (last_tile + tile_group - 1) // tile_group

    def advance(turn_index, running):
        position = turn_index * tile_group + lane_ids
        inside = position < last_tile
        owner_block = jnp.sum((tile_ends[None, :] <= position[:, None]).astype(jnp.int32), axis=1)
        owner_block = jnp.minimum(owner_block, block_count - 1)
        column = jnp.clip(position - tile_starts[owner_block], 0, slot_count - 1)
        partner = nearby[owner_block, column]
        row_side = row_points[:, owner_block]
        col_side = point_halo[:, partner]
        offsets = row_side[:, :, :, None] - col_side[:, :, None, :]
        kernel_tiles = wendland(jnp.sum(offsets * offsets, axis=0)) * inside[:, None, None].astype(
            jnp.float32
        )
        contrib = jnp.einsum(
            "ogn,gmn->ogm", vector_halo[:, partner], kernel_tiles, precision=lax.Precision.HIGHEST
        )
        placing = ((owner_block[:, None] == block_ids[None, :]) & inside[:, None]).astype(
            jnp.float32
        )
        return running + jnp.einsum(
            "ogm,gb->obm", contrib, placing, precision=lax.Precision.HIGHEST
        )

    start_total = jnp.zeros((vector_halo.shape[0], block_count, block_width), jnp.float32)
    return lax.fori_loop(0, turn_count, advance, start_total)


def body(points, targets, landmarks, neighbours, counts, core_inverse):
    col_count = lax.axis_size("cols")
    row_index = lax.axis_index("rows")
    col_index = lax.axis_index("cols")
    block_count = neighbours.shape[0]
    slab_points = points.shape[1]
    block_width = slab_points // block_count
    share_blocks = block_count // col_count
    share_points = share_blocks * block_width
    outputs_count = targets.shape[0]
    reach = 2 * MOST
    first_block = row_index * block_count
    local_ids = landmarks - row_index * slab_points
    present = (local_ids >= 0) & (local_ids < slab_points)
    picked = jnp.take(points, jnp.clip(local_ids, 0, slab_points - 1), axis=1) * present[
        None, :
    ].astype(jnp.float32)
    landmark_coords = lax.psum(picked, "rows")
    share_start = col_index * share_points
    own_points = lax.dynamic_slice_in_dim(points, share_start, share_points, 1)
    landmark_kernel = kernel_scale * wendland(squared_gap(landmark_coords, own_points))

    def precondition_share(residual_share):
        projected = jnp.dot(residual_share, landmark_kernel.T, precision=lax.Precision.HIGHEST)
        projected = lax.psum(projected, ("rows", "cols"))
        weights = jnp.dot(projected, core_inverse, precision=lax.Precision.HIGHEST)
        shared = residual_share - jnp.dot(weights, landmark_kernel, precision=lax.Precision.HIGHEST)
        product = lax.psum(jnp.sum(residual_share * shared, axis=1), ("rows", "cols"))
        return (shared, product)

    point_halo = extended(points, (("rows", 1),), reach * block_width)
    point_halo = point_halo.reshape(3, -1, block_width)
    nearby = neighbours - (first_block - reach)

    def share_of(vector):
        return lax.dynamic_slice_in_dim(vector, share_start, share_points, 1)

    def precondition(residual):
        shared, product = precondition_share(share_of(residual))
        return (lax.all_gather(shared, "cols", axis=1, tiled=True), product)

    solution = jnp.zeros_like(targets)
    residual = targets
    preconditioned, current = precondition(residual)
    direction = preconditioned
    for iteration in range(ITERS):
        vector_halo = extended(direction, (("rows", 1),), reach * block_width)
        vector_halo = vector_halo.reshape(outputs_count, -1, block_width)
        own_lists = lax.dynamic_slice_in_dim(nearby, col_index * share_blocks, share_blocks, 0)
        amounts = lax.dynamic_slice_in_dim(counts, col_index * share_blocks, share_blocks, 0)
        rows_here = own_points.reshape(3, share_blocks, block_width)
        tile_total = jnp.sum(amounts)
        partial_rows = tile_products(
            vector_halo, point_halo, rows_here, own_lists, amounts, tile_total
        )
        operate_product = lax.all_gather(
            partial_rows.reshape(outputs_count, share_points), "cols", axis=1, tiled=True
        )
        applied = kernel_scale * operate_product + ridge_shift * direction
        curvature_part = jnp.sum(share_of(direction) * share_of(applied), axis=1)
        step_size = current / lax.psum(curvature_part, ("rows", "cols"))
        solution = solution + step_size[:, None] * direction
        residual = residual - step_size[:, None] * applied
        if iteration + 1 < ITERS:
            preconditioned, following = precondition(residual)
            direction = preconditioned + (following / current)[:, None] * direction
            current = following
    solution, residual = (solution, residual)
    return (solution, residual)


def solution(mesh):
    placed = (P(None, "rows"), P(None, "rows"), P(), P("rows", None), P("rows"), P())
    return jax.shard_map(
        body,
        mesh=mesh,
        in_specs=placed,
        out_specs=(P(None, "rows"), P(None, "rows")),
        check_vma=False,
    )
```

profile of v0, /device:TPU:1, one launch (start us, length us, event | category | flops | bytes accessed | tf_op | source)
XLA Modules:
  0.0 767.7 jit_solution(12587315131149481955)
XLA Ops:
  0.7 0.8 fusion.98
  1.5 4.8 collective-permute-start
  6.3 1.3 collective-permute-start.1
  7.6 1.5 copy.37
  10.1 121.2 %psum.49 = f32[3,256]{0,1:T(8,128)S(1)} all-reduce(f32[3,256]{0,1:T(8,128)S(1)} %multiply_bitcast_fusion), channel_id=1, replica_groups=mesh['rows'=32,'cols'=16] {'rows'}, use_global_device_ids=true, to_apply=%region_0.1 | all-reduce | flops 768 | bytes 6144 | tf_op jit(solution)/shard_map/psum | solution.py:95
  132.0 124.0 %psum.50 = f32[16,256]{1,0:T(8,128)S(1)} all-reduce(f32[16,256]{1,0:T(8,128)S(1)} %fusion.84), channel_id=1, replica_groups=mesh['rows'=32,'cols'=16] {'rows','cols'}, use_global_device_ids=true, to_apply=%region_2.3 | all-reduce | flops 4096 | bytes 32768 | tf_op jit(solution)/shard_map/psum | solution.py:102
  256.7 16.2 %all_gather.12 = f32[16,4096]{1,0:T(8,128)S(1)} all-gather(f32[16,256]{1,0:T(8,128)S(1)} %get-tuple-element.306), channel_id=1, replica_groups=mesh['rows'=32,'cols'=16] {'cols'}, dimensions={1}, use_global_device_ids=true | all-gather | bytes 278528 | tf_op jit(solution)/shard_map/all_gather | solution.py:117
  272.9 2.8 collective-permute-start.2
  275.7 1.3 collective-permute-start.3
  277.3 0.8 bitcast_subtract_fusion
  279.0 2.5 collective-permute-done.3
  281.6 12.1 %while.22 = (s32[]{:T(128)}, f32[16,2,128]{2,1,0:T(2,128)S(1)}, s32[]{:T(128)}, s32[2]{0:T(128)S(1)}, s32[]{:T(128)}, /*index=5*/f32[3,2,128]{2,0,1:T(4,128)S(1)...) while((s32[]{:T(128)}, f32[16,2,128]{2,1,0:T(2,128)S(1)}, ...), condition=%wide.region_10.11_spmd.clone, body=%wide.region_7.10_spmd.clone.sunk | while | flops 111156288 | bytes 6040561 | solution.py:75
  282.3 1.3 fusion.136
  283.6 0.8 gather_fusion
  287.0 2.1 multiply_reduce_fusion.9
  289.0 4.3 fusion.139
  293.7 16.3 %all_gather.13 = f32[16,4096]{1,0:T(8,128)S(1)} all-gather(f32[16,256]{1,0:T(8,128)S(1)} %bitcast.164), channel_id=1, replica_groups=mesh['rows'=32,'cols'=16] {'cols'}, dimensions={1}, use_global_device_ids=true | all-gather | bytes 278528 | tf_op jit(solution)/shard_map/all_gather | solution.py:133
  310.1 104.1 %all-reduce = (f32[16]{0:T(128)S(1)}, f32[16]{0:T(128)S(1)}) all-reduce(f32[16]{0:T(128)S(1)} %get-tuple-element.305, f32[16]{0:T(128)S(1)} %multiply_reduce_fusion.5), channel_id=1, replica_groups=mesh['rows'=32,'cols'=16] {'rows','cols'}, use_global_device_ids=true, to_apply=%region_4.5 | all-reduce | flops 32 | bytes 256 | tf_op jit(solution)/shard_map/psum | solution.py:105
  414.7 94.7 %psum.53 = f32[16,256]{1,0:T(8,128)S(1)} all-reduce(f32[16,256]{1,0:T(8,128)S(1)} %fusion.82), channel_id=1, replica_groups=mesh['rows'=32,'cols'=16] {'rows','cols'}, use_global_device_ids=true, to_apply=%region_13.14 | all-reduce | flops 4096 | bytes 32768 | tf_op jit(solution)/shard_map/psum | solution.py:102
  510.1 95.3 %psum.54 = f32[16]{0:T(128)S(1)} all-reduce(f32[16]{0:T(128)S(1)} %get-tuple-element.307), channel_id=1, replica_groups=mesh['rows'=32,'cols'=16] {'rows','cols'}, use_global_device_ids=true, to_apply=%region_15.16 | all-reduce | flops 16 | bytes 128 | tf_op jit(solution)/shard_map/psum | solution.py:105
  605.4 18.2 %all_gather.14 = f32[16,4096]{1,0:T(8,128)S(1)} all-gather(f32[16,256]{1,0:T(8,128)S(1)} %get-tuple-element.308), channel_id=1, replica_groups=mesh['rows'=32,'cols'=16] {'cols'}, dimensions={1}, use_global_device_ids=true | all-gather | bytes 278528 | tf_op jit(solution)/shard_map/all_gather | solution.py:117
  623.7 1.7 collective-permute-start.4
  625.4 1.3 collective-permute-start.5
  627.4 4.6 collective-permute-done.5
  632.1 12.0 %while.23 = (s32[]{:T(128)}, f32[16,2,128]{2,1,0:T(2,128)S(1)}, s32[]{:T(128)}, s32[2]{0:T(128)S(1)}, s32[]{:T(128)}, /*index=5*/f32[3,2,128]{2,0,1:T(4,128)S(1)...) while((s32[]{:T(128)}, f32[16,2,128]{2,1,0:T(2,128)S(1)}, ...), condition=%wide.region_19.20_spmd.clone, body=%wide.region_16.19_spmd.clone.sunk | while | flops 111156288 | bytes 6040561 | solution.py:75
  632.8 1.3 fusion.147
  634.1 0.8 gather_fusion.4
  637.4 2.1 multiply_reduce_fusion.10
  639.5 4.3 fusion.150
  644.1 17.1 %all_gather.15 = f32[16,4096]{1,0:T(8,128)S(1)} all-gather(f32[16,256]{1,0:T(8,128)S(1)} %bitcast.165), channel_id=1, replica_groups=mesh['rows'=32,'cols'=16] {'cols'}, dimensions={1}, use_global_device_ids=true | all-gather | bytes 278528 | tf_op jit(solution)/shard_map/all_gather | solution.py:133
  661.4 105.4 %psum.55 = f32[16]{0:T(128)S(1)} all-reduce(f32[16]{0:T(128)S(1)} %multiply_reduce_fusion.3), channel_id=1, replica_groups=mesh['rows'=32,'cols'=16] {'rows','cols'}, use_global_device_ids=true, to_apply=%region_21.22 | all-reduce | flops 16 | bytes 128 | tf_op jit(solution)/shard_map/psum | solution.py:138
  766.8 0.9 multiply_subtract_fusion
  (80 shorter events, 12.1 us)
Async XLA Ops:
  0.6 255.4 %copy-start = (f32[256,256]{1,0:T(8,128)S(1)}, f32[256,256]{1,0:T(8,128)}, u32[]{:S(2)}) copy-start(f32[256,256]{1,0:T(8,128)} %param.15) | copy-start | bytes 786436
  0.6 8.5 %copy-start.1 = (f32[3,4096]{1,0:T(4,128)S(1)}, f32[3,4096]{1,0:T(4,128)}, u32[]{:S(2)}) copy-start(f32[3,4096]{1,0:T(4,128)} %param.10) | copy-start | bytes 147460
  0.7 8.5 %copy-start.4 = (s32[256]{0:T(256)S(1)}, s32[256]{0:T(256)}, u32[]{:S(2)}) copy-start(s32[256]{0:T(256)} %param.12) | copy-start | bytes 3076
  0.7 130.9 %copy-start.2 = (f32[16,4096]{1,0:T(8,128)S(1)}, f32[16,4096]{1,0:T(8,128)}, u32[]{:S(2)}) copy-start(f32[16,4096]{1,0:T(8,128)} %param.11) | copy-start | bytes 786436
  1.5 277.5 %collective-permute-start = (f32[3,1536]{1,0:T(4,128)S(1)}, f32[3,1536]{1,0:T(4,128)S(1)}, u32[]{:S(2)}, u32[]{:S(2)}) collective-permute-start(f32[3,1536]{1,0:T(4,128)S(1)} %get-tuple-element.298), channel_id=1, source_target_pairs={{0,16},{16,32},{32,48},{48,64},{64,80},{80,96},{96,112},{112,128},... | collective-permute-start | bytes 55304 | tf_op jit(solution)/shard_map/ppermute | solution.py:21
  6.3 272.6 %collective-permute-start.1 = (f32[3,1536]{1,0:T(4,128)S(1)}, f32[3,1536]{1,0:T(4,128)S(1)}, u32[]{:S(2)}, u32[]{:S(2)}) collective-permute-start(f32[3,1536]{1,0:T(4,128)S(1)} %get-tuple-element.299), channel_id=1, source_target_pairs={{16,0},{32,16},{48,32},{64,48},{80,64},{96,80},{112,96},{128,112},... | collective-permute-start | bytes 55304 | tf_op jit(solution)/shard_map/ppermute | solution.py:23
  9.1 267.9 %copy-start.5 = (s32[32]{0:T(128)S(1)}, s32[32]{0:T(128)}, u32[]{:S(2)}) copy-start(s32[32]{0:T(128)} %param.14) | copy-start | bytes 388
  9.1 269.0 %copy-start.3 = (s32[32,18]{0,1:T(8,128)S(1)}, s32[32,18]{0,1:T(8,128)}, u32[]{:S(2)}) copy-start(s32[32,18]{0,1:T(8,128)} %param.13) | copy-start | bytes 6916
  272.9 6.1 collective-permute-start.2
  275.7 5.8 collective-permute-start.3
  623.7 3.6 collective-permute-start.4
  625.4 6.6 collective-permute-start.5
where the time goes:
time: 769 us; the launch traced here: 768 us
  blocking collectives  713 us (93%)
  starting transfers between devices  13.1 us (2%)
  matrix products  11.3 us (1%)
  other arithmetic  11.2 us (1%)
  local copies, waits for them, and re-layouts  9.75 us (1%)
  waiting for transfers between devices  7.82 us (1%)
    psum x2, blocking collectives, precondition_share(): projected = lax.psum(projected, ('rows', 'cols'))  219 us
    psum x2, blocking collectives, precondition_share(): lax.psum(jnp.sum(residual_share * shared, axis=1), ('rows', 'cols'))  199 us
    psum x1, blocking collectives, body(): landmark_coords = lax.psum(picked, 'rows')  121 us
    psum x1, blocking collectives, body(): step_size = current / lax.psum(curvature_part, ('rows', 'cols'))  105 us
    all_gather x2, blocking collectives, precondition(): return (lax.all_gather(shared, 'cols', axis=1, tiled=True), product)  34.4 us
    all_gather x2, blocking collectives, body(): lax.all_gather(partial_rows.reshape(outputs_count, share_points), 'cols',...  33.5 us
  transfers between devices with their start and end apart: 6, of which 3 were waited for; matrix products, arithmetic and copies ran while one was open for 1% of the time, Pallas kernels for 0%

commit v1 on v0

--- a/solution.py
+++ b/solution.py
@@ -114,7 +114,19 @@
 
     def precondition(residual):
         shared, product = precondition_share(share_of(residual))
-        return (lax.all_gather(shared, "cols", axis=1, tiled=True), product)
+
+        def _feed_islands(xin, k_dim=1):
+            return jnp.concatenate(
+                lax.all_to_all(
+                    jnp.stack(lax.axis_size("cols") * [xin]),
+                    axis_name="cols",
+                    split_axis=0,
+                    concat_axis=0,
+                ),
+                axis=k_dim,
+            )
+
+        return (_feed_islands(shared), product)
 
     solution = jnp.zeros_like(targets)
     residual = targets

time: 769 us -> 762 us (level)
  blocking collectives: 713 us -> 682 us
  starting transfers between devices: 13.1 us -> 24.7 us
  waiting for transfers between devices: 7.82 us -> 19 us
    all_gather x2 -> x0, blocking collectives: 34.4 us -> none  [precondition(): return (lax.all_gather(shared, 'cols', axis=1, tiled=True), product)]
    all_to_all x0 -> x2, starting transfers between devices: none -> 10.2 us  [_feed_islands(): lax.all_to_all(jnp.stack(lax.axis_size('cols') * [xin]), axis_name='cols'...]
    all_to_all x0 -> x2, waiting for transfers between devices: none -> 9.64 us  [_feed_islands(): lax.all_to_all(jnp.stack(lax.axis_size('cols') * [xin]), axis_name='cols'...]
  transfers between devices with their start and end apart: 6 -> 8, of which waited for: 3 -> 5; matrix products, arithmetic and copies ran while one was open for 1% -> 1% of each run, Pallas kernels for 0% -> 0%
where the time goes in v1:
time: 762 us; the launch traced here: 761 us
  blocking collectives  682 us (90%)
  starting transfers between devices  24.7 us (3%)
  waiting for transfers between devices  19 us (2%)
  local copies, waits for them, and re-layouts  11.3 us (1%)
  matrix products  11.3 us (1%)
  other arithmetic  11.2 us (1%)
    psum x2, blocking collectives, precondition_share(): projected = lax.psum(projected, ('rows', 'cols'))  219 us
    psum x2, blocking collectives, precondition_share(): lax.psum(jnp.sum(residual_share * shared, axis=1), ('rows', 'cols'))  201 us
    psum x1, blocking collectives, body(): landmark_coords = lax.psum(picked, 'rows')  121 us
    psum x1, blocking collectives, body(): step_size = current / lax.psum(curvature_part, ('rows', 'cols'))  107 us
    all_gather x2, blocking collectives, body(): lax.all_gather(partial_rows.reshape(outputs_count, share_points), 'cols',...  33.2 us
  transfers between devices with their start and end apart: 8, of which 5 were waited for; matrix products, arithmetic and copies ran while one was open for 1% of the time, Pallas kernels for 0%

profile of v1, /device:TPU:1, one launch (start us, length us, event | category | flops | bytes accessed | tf_op | source)
XLA Modules:
  0.0 761.1 jit_solution(17470522865485707253)
XLA Ops:
  0.7 0.8 fusion.98
  1.5 4.8 collective-permute-start
  6.3 1.3 collective-permute-start.1
  7.6 1.5 copy.52
  10.1 121.2 %psum.49 = f32[3,256]{0,1:T(8,128)S(1)} all-reduce(f32[3,256]{0,1:T(8,128)S(1)} %multiply_bitcast_fusion), channel_id=1, replica_groups=mesh['rows'=32,'cols'=16] {'rows'}, use_global_device_ids=true, to_apply=%region_0.1 | all-reduce | flops 768 | bytes 6144 | tf_op jit(solution)/shard_map/psum | solution.py:95
  132.0 124.0 %psum.50 = f32[16,256]{1,0:T(8,128)S(1)} all-reduce(f32[16,256]{1,0:T(8,128)S(1)} %fusion.84), channel_id=1, replica_groups=mesh['rows'=32,'cols'=16] {'rows','cols'}, use_global_device_ids=true, to_apply=%region_2.3 | all-reduce | flops 4096 | bytes 32768 | tf_op jit(solution)/shard_map/psum | solution.py:102
  257.4 4.5 all-to-all-start
  262.2 0.8 bitcast_subtract_fusion
  263.9 9.6 %all-to-all-done = f32[16,16,256]{2,1,0:T(8,128)S(1)} async-done(((f32[16,16,256]{2,1,0:T(8,128)}), f32[16,16,256]{2,1,0:T(8,128)S(1)}, u32[]{:S(2)}, u32[]{:S(2)}) %all-to-all-start) | async-done | bytes 262176 | tf_op jit(solution)/shard_map/all_to_all | solution.py:120
  273.6 3.0 collective-permute-start.2
  276.6 1.3 collective-permute-start.3
  277.9 1.1 collective-permute-done.2
  279.1 3.8 collective-permute-done.3
  283.0 12.1 %while.22 = (s32[]{:T(128)}, f32[16,2,128]{2,1,0:T(2,128)S(1)}, s32[]{:T(128)}, s32[2]{0:T(128)S(1)}, s32[]{:T(128)}, /*index=5*/f32[3,2,128]{2,0,1:T(4,128)S(1)...) while((s32[]{:T(128)}, f32[16,2,128]{2,1,0:T(2,128)S(1)}, ...), condition=%wide.region_10.11_spmd.clone, body=%wide.region_7.10_spmd.clone.sunk | while | flops 111156288 | bytes 6040561 | solution.py:75
  283.7 1.3 fusion.136
  288.3 2.1 multiply_reduce_fusion.9
  290.4 4.3 fusion.139
  295.1 15.5 %all_gather.6 = f32[16,4096]{1,0:T(8,128)S(1)} all-gather(f32[16,256]{1,0:T(8,128)S(1)} %bitcast.179), channel_id=1, replica_groups=mesh['rows'=32,'cols'=16] {'cols'}, dimensions={1}, use_global_device_ids=true | all-gather | bytes 278528 | tf_op jit(solution)/shard_map/all_gather | solution.py:145
  310.7 103.5 %all-reduce = (f32[16]{0:T(128)S(1)}, f32[16]{0:T(128)S(1)}) all-reduce(f32[16]{0:T(128)S(1)} %get-tuple-element.325, f32[16]{0:T(128)S(1)} %multiply_reduce_fusion.5), channel_id=1, replica_groups=mesh['rows'=32,'cols'=16] {'rows','cols'}, use_global_device_ids=true, to_apply=%region_4.5 | all-reduce | flops 32 | bytes 256 | tf_op jit(solution)/shard_map/psum | solution.py:105
  414.7 94.7 %psum.53 = f32[16,256]{1,0:T(8,128)S(1)} all-reduce(f32[16,256]{1,0:T(8,128)S(1)} %fusion.82), channel_id=1, replica_groups=mesh['rows'=32,'cols'=16] {'rows','cols'}, use_global_device_ids=true, to_apply=%region_13.14 | all-reduce | flops 4096 | bytes 32768 | tf_op jit(solution)/shard_map/psum | solution.py:102
  510.8 5.7 all-to-all-start.1
  516.5 97.8 %psum.54 = f32[16]{0:T(128)S(1)} all-reduce(f32[16]{0:T(128)S(1)} %get-tuple-element.327), channel_id=1, replica_groups=mesh['rows'=32,'cols'=16] {'rows','cols'}, use_global_device_ids=true, to_apply=%region_15.16 | all-reduce | flops 16 | bytes 128 | tf_op jit(solution)/shard_map/psum | solution.py:105
  614.5 2.8 collective-permute-start.4
  617.2 1.3 collective-permute-start.5
  618.9 4.0 collective-permute-done.5
  622.9 12.0 %while.23 = (s32[]{:T(128)}, f32[16,2,128]{2,1,0:T(2,128)S(1)}, s32[]{:T(128)}, s32[2]{0:T(128)S(1)}, s32[]{:T(128)}, /*index=5*/f32[3,2,128]{2,0,1:T(4,128)S(1)...) while((s32[]{:T(128)}, f32[16,2,128]{2,1,0:T(2,128)S(1)}, ...), condition=%wide.region_19.20_spmd.clone, body=%wide.region_16.19_spmd.clone.sunk | while | flops 111156288 | bytes 6040561 | solution.py:75
  623.7 1.3 fusion.147
  628.3 2.1 multiply_reduce_fusion.10
  630.4 4.3 fusion.150
  635.0 17.7 %all_gather.7 = f32[16,4096]{1,0:T(8,128)S(1)} all-gather(f32[16,256]{1,0:T(8,128)S(1)} %bitcast.180), channel_id=1, replica_groups=mesh['rows'=32,'cols'=16] {'cols'}, dimensions={1}, use_global_device_ids=true | all-gather | bytes 278528 | tf_op jit(solution)/shard_map/all_gather | solution.py:145
  652.8 107.3 %psum.55 = f32[16]{0:T(128)S(1)} all-reduce(f32[16]{0:T(128)S(1)} %multiply_reduce_fusion.3), channel_id=1, replica_groups=mesh['rows'=32,'cols'=16] {'rows','cols'}, use_global_device_ids=true, to_apply=%region_21.22 | all-reduce | flops 16 | bytes 128 | tf_op jit(solution)/shard_map/psum | solution.py:150
  760.2 0.9 multiply_subtract_fusion
  (86 shorter events, 14.8 us)
Async XLA Ops:
  0.6 255.4 %copy-start = (f32[256,256]{1,0:T(8,128)S(1)}, f32[256,256]{1,0:T(8,128)}, u32[]{:S(2)}) copy-start(f32[256,256]{1,0:T(8,128)} %param.15) | copy-start | bytes 786436
  0.6 8.5 %copy-start.1 = (f32[3,4096]{1,0:T(4,128)S(1)}, f32[3,4096]{1,0:T(4,128)}, u32[]{:S(2)}) copy-start(f32[3,4096]{1,0:T(4,128)} %param.10) | copy-start | bytes 147460
  0.7 8.5 %copy-start.4 = (s32[256]{0:T(256)S(1)}, s32[256]{0:T(256)}, u32[]{:S(2)}) copy-start(s32[256]{0:T(256)} %param.12) | copy-start | bytes 3076
  0.7 130.9 %copy-start.2 = (f32[16,4096]{1,0:T(8,128)S(1)}, f32[16,4096]{1,0:T(8,128)}, u32[]{:S(2)}) copy-start(f32[16,4096]{1,0:T(8,128)} %param.11) | copy-start | bytes 786436
  1.5 276.4 %collective-permute-start = (f32[3,1536]{1,0:T(4,128)S(1)}, f32[3,1536]{1,0:T(4,128)S(1)}, u32[]{:S(2)}, u32[]{:S(2)}) collective-permute-start(f32[3,1536]{1,0:T(4,128)S(1)} %get-tuple-element.318), channel_id=1, source_target_pairs={{0,16},{16,32},{32,48},{48,64},{64,80},{80,96},{96,112},{112,128},... | collective-permute-start | bytes 55304 | tf_op jit(solution)/shard_map/ppermute | solution.py:21
  6.3 271.6 %collective-permute-start.1 = (f32[3,1536]{1,0:T(4,128)S(1)}, f32[3,1536]{1,0:T(4,128)S(1)}, u32[]{:S(2)}, u32[]{:S(2)}) collective-permute-start(f32[3,1536]{1,0:T(4,128)S(1)} %get-tuple-element.319), channel_id=1, source_target_pairs={{16,0},{32,16},{48,32},{64,48},{80,64},{96,80},{112,96},{128,112},... | collective-permute-start | bytes 55304 | tf_op jit(solution)/shard_map/ppermute | solution.py:23
  9.1 252.8 %copy-start.5 = (s32[32]{0:T(128)S(1)}, s32[32]{0:T(128)}, u32[]{:S(2)}) copy-start(s32[32]{0:T(128)} %param.14) | copy-start | bytes 388
  9.1 254.6 %copy-start.3 = (s32[32,18]{0,1:T(8,128)S(1)}, s32[32,18]{0,1:T(8,128)}, u32[]{:S(2)}) copy-start(s32[32,18]{0,1:T(8,128)} %param.13) | copy-start | bytes 6916
  257.4 16.1 %all-to-all-start = ((f32[16,16,256]{2,1,0:T(8,128)}), f32[16,16,256]{2,1,0:T(8,128)S(1)}, u32[]{:S(2)}, u32[]{:S(2)}) async-start(f32[16,16,256]{2,1,0:T(8,128)} %stack.4), calls=%async_computation | async-start | bytes 524288 | tf_op jit(solution)/shard_map/all_to_all | solution.py:120
  273.6 5.5 collective-permute-start.2
  276.6 6.3 collective-permute-start.3
  510.8 103.6 %all-to-all-start.1 = ((f32[16,16,256]{2,1,0:T(8,128)}), f32[16,16,256]{2,1,0:T(8,128)S(1)}, u32[]{:S(2)}, u32[]{:S(2)}) async-start(f32[16,16,256]{2,1,0:T(8,128)} %stack.5), calls=%async_computation.1 | async-start | bytes 524288 | tf_op jit(solution)/shard_map/all_to_all | solution.py:120
  614.5 4.4 collective-permute-start.4
  617.2 5.7 collective-permute-start.5
